TPU v7x, 128 devices: a whole 4x4x4 slice. The times are simulated.
128 devices in a mesh: dp: 2 (over z_hi), seq: 32 (over y, x, core), tensor: 2 (over z_lo).
Axes of the slice: x: 4, y: 4, z: 4 (z_hi: 2, z_lo: 2; z = z_hi * 2 + z_lo), core: 2. Of those that a mesh axis runs over, the one named last changes fastest.
Arguments:
- queries: bfloat16 [2, 16384, 4096], P('dp', 'seq', 'tensor'), may hold values from -6 to 6
- keys: bfloat16 [2, 16384, 4096], P('dp', 'seq', 'tensor'), may hold values from -6 to 6
- values: bfloat16 [2, 16384, 4096], P('dp', 'seq', 'tensor'), may hold values from -40 to 40
- grad_out: bfloat16 [2, 16384, 4096], P('dp', 'seq', 'tensor'), may hold values from -48 to 48
- doc_lengths: int32 [2, 16], P('dp'), may hold values from 1 to 9216, 16384 in all within a row
- gain: float32 [4096], P('tensor'), may hold values from 0.1 to 1.9
Outputs:
- layer_out: bfloat16 [2, 16384, 4096], P('dp', 'seq', 'tensor')
- grad_queries: bfloat16 [2, 16384, 4096], P('dp', 'seq', 'tensor')
- grad_keys: bfloat16 [2, 16384, 4096], P('dp', 'seq', 'tensor')
- grad_values: bfloat16 [2, 16384, 4096], P('dp', 'seq', 'tensor')
- grad_gain: float32 [4096], P('tensor')
Inputs may be any that keep to these rules, and one draw needn't show every extreme that they name: `doc_lengths`: each row sums to 16384; in every sequence the longest document has exactly 9216 tokens.
All inputs are finite; a program needn't handle non-finite values.
Results may differ from a plain program's by a relative error of at most 0.0063.
Values may be sent and summed in bfloat16 or wider, within the bound.
No kernel may reach another device: no remote copies, remote signals or barrier semaphores. Data moves between devices by JAX's collectives and lax.ppermute only.
A program may use at most 128 MiB of HBM per device.

v0:
```python
import jax
import jax.numpy as jnp
from jax import lax
from jax.sharding import PartitionSpec as P

HEADS = 32
HD = 128
epsilon = 1e-05


def prefix(value, axis, join, neutral, backward):
    count = lax.axis_size(axis)
    place = lax.axis_index(axis)
    ahead = count - 1 - place if backward else place
    gathered = jax.tree.map(
        lambda a, kind: lax.all_gather(a.astype(kind), axis), value, (jnp.bfloat16, jnp.bfloat16)
    )
    state = jax.tree.map(lambda a, e: jnp.zeros_like(a) + jnp.asarray(e, a.dtype), value, neutral)

    def one(step, state):
        source = count - 1 - step if backward else step
        return join(
            state,
            jax.tree.map(
                lambda a, own: lax.dynamic_index_in_dim(a, source, 0, False).astype(own.dtype),
                gathered,
                value,
            ),
        )

    return lax.fori_loop(0, ahead, one, state)


def linked(earlier, later):
    keeping = 1.0 - later[1][0]
    return (later[0] + keeping * earlier[0], jnp.maximum(earlier[1], later[1]))


def carried(state, flags, backward):
    blank = jnp.zeros(state.shape, jnp.float32)
    total, unused = prefix(
        (state.astype(jnp.float32), flags),
        "seq",
        linked,
        (blank, jnp.zeros((1,), jnp.float32)),
        backward,
    )
    return total


def head_major(array, shape):
    return jnp.transpose(array.reshape(shape), (1, 0, 2))


def body(queries, keys, values, grad_out, doc_lengths, gain):
    count = queries.shape[1]
    local_width = queries.shape[2]
    local_heads = local_width // HD
    shape = (count, local_heads, HD)
    query = head_major(queries[0], shape)
    key = head_major(keys[0], shape)
    value = head_major(values[0], shape)
    lengths = doc_lengths[0]
    starts = jnp.cumsum(lengths) - lengths
    block = lax.axis_index("seq")
    begin = block * count
    position = begin + jnp.arange(count, dtype=jnp.int32)
    document = jnp.sum((starts[None, :] <= position[:, None]).astype(jnp.int32), axis=1) - 1
    first_doc = document[0]
    last_doc = document[-1]
    numbers = jnp.arange(starts.shape[0], dtype=jnp.int32)
    last_end = jnp.sum(jnp.where(numbers == last_doc, starts + lengths, 0))
    last_block = (last_end - 1) // count
    continues = jnp.logical_not(jnp.any(starts == begin))
    starts_here = jnp.any((starts >= begin) & (starts < begin + count))
    flags = starts_here.astype(jnp.float32).reshape(1)
    first_mask = (document == first_doc) & continues
    last_mask = document == last_doc
    indices = jnp.arange(count, dtype=jnp.int32)
    same = (indices[:, None] >= indices[None, :]) & (document[:, None] == document[None, :])
    key_last = jnp.where(last_mask[None, :, None], key, 0)
    value_last = jnp.where(last_mask[None, :, None], value, 0)
    query_first = jnp.where(first_mask[None, :, None], query, 0)
    state = jnp.einsum("htd,hte->hde", key_last, value, preferred_element_type=jnp.float32).astype(
        jnp.bfloat16
    )
    incoming = carried(state, flags, False)
    carry_in = jnp.where(continues, incoming, 0.0).astype(jnp.bfloat16)
    scores = jnp.einsum("htd,hsd->hts", query, key, preferred_element_type=jnp.float32)
    scores = jnp.where(same[None], scores, 0.0).astype(jnp.bfloat16)
    attended = jnp.einsum("hts,hsd->htd", scores, value, preferred_element_type=jnp.float32)
    attended = attended + jnp.einsum(
        "htd,hde->hte", query_first, carry_in, preferred_element_type=jnp.float32
    )
    attended = jnp.transpose(attended, (1, 0, 2)).reshape(count, local_width)
    squares = lax.psum(jnp.sum(attended * attended, axis=1), "tensor")
    rscale = lax.rsqrt(squares / (HEADS * HD) + epsilon)
    unit = attended * rscale[:, None]
    layer_out = (gain * unit).astype(jnp.bfloat16)
    upstream = grad_out[0].astype(jnp.float32)
    scaled = upstream * gain
    inner = lax.psum(jnp.sum(scaled * unit, axis=1), "tensor") / (HEADS * HD)
    grad_gain = lax.psum(jnp.sum(upstream * unit, axis=0), ("dp", "seq"))
    d_att = head_major(
        (rscale[:, None] * (scaled - unit * inner[:, None])).astype(jnp.bfloat16), shape
    )
    d_first = jnp.where(first_mask[None, :, None], d_att, 0)
    back_state = jnp.einsum(
        "htd,hte->hde", query_first, d_att, preferred_element_type=jnp.float32
    ).astype(jnp.bfloat16)
    outgoing = carried(back_state, flags, True)
    carry_back = jnp.where(last_block > block, outgoing, 0.0).astype(jnp.bfloat16)
    d_scores = jnp.einsum("hte,hse->hts", d_att, value, preferred_element_type=jnp.float32)
    d_scores = jnp.where(same[None], d_scores, 0.0).astype(jnp.bfloat16)
    grad_query = jnp.einsum("hts,hsd->htd", d_scores, key, preferred_element_type=jnp.float32)
    grad_query = grad_query + jnp.einsum(
        "hte,hde->htd", d_first, carry_in, preferred_element_type=jnp.float32
    )
    grad_key = jnp.einsum("hts,htd->hsd", d_scores, query, preferred_element_type=jnp.float32)
    grad_key = grad_key + jnp.einsum(
        "hse,hde->hsd", value_last, carry_back, preferred_element_type=jnp.float32
    )
    grad_value = jnp.einsum("hts,hte->hse", scores, d_att, preferred_element_type=jnp.float32)
    grad_value = grad_value + jnp.einsum(
        "hsd,hde->hse", key_last, carry_back, preferred_element_type=jnp.float32
    )
    out_shape = (1, count, local_width)

    def token_major(array):
        return jnp.transpose(array.astype(jnp.bfloat16), (1, 0, 2)).reshape(out_shape)

    return (
        layer_out.reshape(out_shape),
        token_major(grad_query),
        token_major(grad_key),
        token_major(grad_value),
        grad_gain,
    )


def solution(mesh):
    in_specs = (
        P("dp", "seq", "tensor"),
        P("dp", "seq", "tensor"),
        P("dp", "seq", "tensor"),
        P("dp", "seq", "tensor"),
        P("dp", None),
        P("tensor"),
    )
    out_specs = (
        P("dp", "seq", "tensor"),
        P("dp", "seq", "tensor"),
        P("dp", "seq", "tensor"),
        P("dp", "seq", "tensor"),
        P("tensor"),
    )
    return jax.shard_map(body, mesh=mesh, in_specs=in_specs, out_specs=out_specs, check_vma=False)
```

profile of v0, /device:TPU:0, one launch (start us, length us, event | category | flops | bytes accessed | tf_op | source)
XLA Modules:
  0.0 547.0 jit_solution(15308874766064887949)
XLA Ops:
  11.5 3.9 copy.79
  24.8 69.2 %all-reduce = bf16[32]{0:T(256)(128)(2,1)S(1)} all-reduce(bf16[32]{0:T(256)(128)(2,1)S(1)} %dynamic-update-slice), channel_id=1, replica_groups=mesh['dp'=2,'seq'=32,'tensor'=2] {'seq'}, use_global_device_ids=true, to_apply=%add | all-reduce | flops 32 | bytes 128
  97.0 4.1 copy.87
  101.3 4.2 select_convert_fusion.1
  108.7 4.8 fusion.40
  113.6 5.0 fusion.7
  118.6 5.0 psum.21
  123.6 5.4 copy.88
  129.0 4.0 fusion.2
  133.0 5.1 psum.22
  138.2 4.3 fusion.8
  147.3 5.4 copy.86
  152.7 4.8 select_convert_fusion
  157.6 4.8 fusion.41
  162.4 4.3 add_convert_fusion.2
  166.7 3.9 copy.96
  170.6 252.2 %psum.23 = f32[2048]{0:T(1024)} all-reduce(f32[2048]{0:T(1024)S(1)} %get-tuple-element.155), channel_id=1, replica_groups=mesh['dp'=2,'seq'=32,'tensor'=2] {'dp','seq'}, use_global_device_ids=true, to_apply=%region_14.15 | all-reduce | flops 2048 | bytes 16384 | tf_op jit(solution)/shard_map/psum | solution.py:103
  422.8 3.9 multiply_convert_fusion
  426.7 6.7 %fusion.42 = f32[16,512,128]{1,2,0:T(8,128)} fusion(bf16[16,512,128]{1,2,0:T(8,128)(2,1)S(1)} %bitcast.105, bf16[16,512,512]{2,1,0:T(8,128)(2,1)} %copy-done), kind=kOutput, calls=%fused_computation.74 | convolution fusion | flops 1073741824 | bytes 14680064 | tf_op jit(solution)/shard_map/hts,htd->hsd/dot_general | solution.py:119
  433.5 86.6 %while.27 = (s32[]{:T(128)}, f32[16,128,128]{2,1,0:T(8,128)S(1)}, s32[]{:T(128)}, bf16[32,16,128,128]{3,2,1,0:T(8,128)(2,1)}, bf16[32,1]{0,1:T(2,128)(2,1)S(1)},...) while((s32[]{:T(128)}, f32[16,128,128]{2,1,0:T(8,128)S(1)}, s32[]{:T(128)}, ...), condition=%wide.region_12.13_spmd, body=%wide.region_11.12_spmd.sunk | while | flops 786439 | bytes 2621605 | solution.py:31
  521.8 6.2 %add_convert_fusion = bf16[16,512,128]{1,2,0:T(8,128)(2,1)} fusion(f32[16,512,128]{1,2,0:T(8,128)S(1)} %fusion.14, bf16[16,512,128]{1,2,0:T(8,128)(2,1)S(1)} %copy-done.9, bf16[16,512,512]{2,1,0:T(8,128)(2,1)} %copy-done.1), kind=kOutput, calls=%fused_computation.18 | convolution fusion | flops 1075838976 | bytes 16777216 | tf_op jit(solution)/shard_map/hts,hte->hse/dot_general | solution.py:123
  528.0 4.1 copy.98
  532.1 4.2 add_convert_fusion.1
  536.3 3.9 copy.97
  (117 shorter events, 110.4 us)
Async XLA Ops:
  7.2 106.3 %all-gather.5.cloned.1.call-start = ((), (), s32[]{:S(2)}) async-start(), calls=%async_computation | async-start | bytes 17301504 | tf_op jit(solution)/shard_map/all_gather | solution.py:16
  18.3 4.5 copy-start.2
  19.6 3.9 copy-start.11
  22.8 410.6 %all-gather.7.cloned.1.call-start = ((), (), s32[]{:S(2)}) async-start(), calls=%async_computation.1 | async-start | bytes 17301504 | tf_op jit(solution)/shard_map/all_gather | solution.py:16
  101.3 7.4 %copy-start.3 = (bf16[1,512,2048]{1,2,0:T(8,128)(2,1)S(1)}, bf16[1,512,2048]{1,2,0:T(8,128)(2,1)}, u32[]{:S(2)}) copy-start(bf16[1,512,2048]{1,2,0:T(8,128)(2,1)} %copy-done.2) | copy-start | bytes 6291460
  105.5 3.2 copy-start.1
  123.6 5.4 copy-start.10
  142.4 1.4 copy-start.7
  152.7 4.8 copy-start.5
  157.6 4.8 copy-start
  157.6 4.8 copy-start.8
  433.5 86.7 %copy-start.6 = (bf16[1,512,2048]{1,2,0:T(8,128)(2,1)S(1)}, bf16[1,512,2048]{1,2,0:T(8,128)(2,1)}, u32[]{:S(2)}) copy-start(bf16[1,512,2048]{1,2,0:T(8,128)(2,1)} %copy.79) | copy-start | bytes 6291460
  520.2 1.6 copy-start.9
  528.0 4.1 copy-start.4
Sparse Core Ops, SparseCore 0:
  22.9 75.2 all-gather.4
  145.5 151.3 all-gather.6
where the time goes:
time: 550 us; the launch traced here: 547 us
  blocking collectives  332 us (60%)
  other arithmetic  103 us (19%)
  matrix products  50.3 us (9%)
  local copies, waits for them, and re-layouts  44.8 us (8%)
  between operations  16.2 us (3%)
    psum x1, blocking collectives, body(): grad_gain = lax.psum(jnp.sum(upstream * unit, axis=0), ('dp', 'seq'))  252 us
    unnamed x1, blocking collectives  69.2 us
    add x31, other arithmetic, linked(): return (later[0] + keeping * earlier[0], jnp.maximum(earlier[1], later[1]))  65.4 us
    unnamed x33, local copies, waits for them, and re-layouts  28.3 us
    sub x31, other arithmetic, linked(): keeping = 1.0 - later[1][0]  20.3 us
  transfers between devices with their start and end apart: 2, of which 0 were waited for; matrix products, arithmetic and copies ran while one was open for 10% of the time, Pallas kernels for 0%

commit v1 on v0

--- a/solution.py
+++ b/solution.py
@@ -100,7 +100,7 @@
     upstream = grad_out[0].astype(jnp.float32)
     scaled = upstream * gain
     inner = lax.psum(jnp.sum(scaled * unit, axis=1), "tensor") / (HEADS * HD)
-    grad_gain = lax.psum(jnp.sum(upstream * unit, axis=0), ("dp", "seq"))
+    grad_gain = lax.psum(lax.psum(jnp.sum(upstream * unit, axis=0), "dp"), "seq")
     d_att = head_major(
         (rscale[:, None] * (scaled - unit * inner[:, None])).astype(jnp.bfloat16), shape
     )

time: 550 us -> 452 us (0.82)
  blocking collectives: 332 us -> 234 us
    psum x1 -> x2, blocking collectives: 252 us -> 155 us  [the longest x1 148 us: body(): lax.psum(lax.psum(jnp.sum(upstream * unit, axis=0), 'dp'), 'seq')]
  transfers between devices with their start and end apart: 2 -> 2, of which waited for: 0 -> 0; matrix products, arithmetic and copies ran while one was open for 10% -> 12% of each run, Pallas kernels for 0% -> 0%
where the time goes in v1:
time: 452 us; the launch traced here: 449 us
  blocking collectives  234 us (52%)
  other arithmetic  103 us (23%)
  matrix products  50.3 us (11%)
  local copies, waits for them, and re-layouts  44.8 us (10%)
  between operations  16.2 us (4%)
    psum x1, blocking collectives, body(): lax.psum(lax.psum(jnp.sum(upstream * unit, axis=0), 'dp'), 'seq')  148 us
    unnamed x1, blocking collectives  69.2 us
    add x31, other arithmetic, linked(): return (later[0] + keeping * earlier[0], jnp.maximum(earlier[1], later[1]))  65.4 us
    unnamed x33, local copies, waits for them, and re-layouts  28.3 us
    sub x31, other arithmetic, linked(): keeping = 1.0 - later[1][0]  20.3 us
    reshape x2, local copies, waits for them, and re-layouts, body(): attended = jnp.transpose(attended, (1, 0, 2)).reshape(count, local_width)  10.8 us
  transfers between devices with their start and end apart: 2, of which 0 were waited for; matrix products, arithmetic and copies ran while one was open for 12% of the time, Pallas kernels for 0%

profile of v1, /device:TPU:0, one launch (start us, length us, event | category | flops | bytes accessed | tf_op | source)
XLA Modules:
  0.0 449.3 jit_solution(9760307638735278861)
XLA Ops:
  11.5 3.9 copy.79
  24.8 69.2 %all-reduce = bf16[32]{0:T(256)(128)(2,1)S(1)} all-reduce(bf16[32]{0:T(256)(128)(2,1)S(1)} %dynamic-update-slice), channel_id=1, replica_groups=mesh['dp'=2,'seq'=32,'tensor'=2] {'seq'}, use_global_device_ids=true, to_apply=%add | all-reduce | flops 32 | bytes 128
  97.0 4.1 copy.87
  101.3 4.2 select_convert_fusion.1
  108.7 4.8 %fusion.40 = f32[16,512,128]{1,2,0:T(8,128)} fusion(bf16[16,512,512]{2,1,0:T(8,128)(2,1)S(1)} %select_convert_fusion.1, bf16[16,512,128]{1,2,0:T(8,128)(2,1)S(1)} %bitcast.108), kind=kOutput, calls=%fused_computation.72 | convolution fusion | flops 1073741824 | bytes 14680064 | tf_op jit(solution)/shard_map/hts,hsd->htd/dot_general | solution.py:91
  113.6 5.0 %fusion.7 = (f32[512]{0:T(512)S(1)}, f32[16,512,128]{1,2,0:T(8,128)}) fusion(f32[16,512,128]{1,2,0:T(8,128)} %fusion.40, f32[16,128,128]{2,1,0:T(8,128)S(1)} %get-tuple-element.133, pred[]{:T(512)S(6)} %not.3, bf16[16,512,128]{1,2,0:T(8,128)(2,1)S(1)} %bitcast.103, pred[512]{0:T(512)(128)(4,1)S(1)} %get-tuple-element.180), kind=kOutput, calls=%fused_computation.17 | convolution fusion | flops 272891392 | bytes 11536897 | tf_op jit(solution)/shard_map/htd,hde->hte/dot_general | solution.py:92
  118.6 5.0 %psum.28 = f32[512]{0:T(512)S(1)} all-reduce(f32[512]{0:T(512)S(1)} %get-tuple-element.183), channel_id=1, replica_groups=mesh['dp'=2,'seq'=32,'tensor'=2] {'tensor'}, use_global_device_ids=true, to_apply=%region_7.8 | all-reduce | flops 512 | bytes 4096 | tf_op jit(solution)/shard_map/psum | solution.py:96
  123.6 5.4 %copy.88 = f32[512,2048]{1,0:T(8,128)} copy(f32[512,2048]{0,1:T(8,128)} %bitcast.100) | data formatting | bytes 8388608 | tf_op jit(solution)/shard_map/reshape | solution.py:95
  129.0 4.0 fusion.2
  133.0 5.1 %psum.29 = f32[512]{0:T(512)S(1)} all-reduce(f32[512]{0:T(512)S(1)} %get-tuple-element.156), channel_id=1, replica_groups=mesh['dp'=2,'seq'=32,'tensor'=2] {'tensor'}, use_global_device_ids=true, to_apply=%region_9.10 | all-reduce | flops 512 | bytes 4096 | tf_op jit(solution)/shard_map/psum | solution.py:102
  138.2 4.3 fusion.8
  147.3 5.4 %copy.86 = f32[1,512,2048]{2,1,0:T(8,128)} copy(f32[1,512,2048]{1,2,0:T(8,128)} %bitcast.101) | data formatting | bytes 8388608 | tf_op jit(solution)/shard_map/reshape | solution.py:95
  152.7 4.8 %select_convert_fusion = bf16[16,512,512]{2,1,0:T(8,128)(2,1)S(1)} fusion(bf16[16,512,128]{1,2,0:T(8,128)(2,1)} %copy-done.7, bf16[16,512,128]{1,2,0:T(8,128)(2,1)} %bitcast.107, pred[512,512]{1,0:T(8,128)(4,1)S(1)} %fusion.24), kind=kOutput, calls=%fused_computation.4 | convolution fusion | flops 1082130432 | bytes 12845056 | tf_op jit(solution)/shard_map/hte,hse->hts/dot_general | solution.py:113
  157.6 4.8 %fusion.41 = f32[16,512,128]{1,2,0:T(8,128)} fusion(bf16[16,512,512]{2,1,0:T(8,128)(2,1)S(1)} %select_convert_fusion, bf16[16,512,128]{1,2,0:T(8,128)(2,1)S(1)} %bitcast.112), kind=kOutput, calls=%fused_computation.73 | convolution fusion | flops 1073741824 | bytes 14680064 | tf_op jit(solution)/shard_map/hts,hsd->htd/dot_general | solution.py:115
  162.4 4.3 add_convert_fusion.2
  166.7 3.9 copy.96
  170.6 7.0 %psum.30 = f32[2048]{0:T(1024)S(1)} all-reduce(f32[2048]{0:T(1024)S(1)} %get-tuple-element.155), channel_id=1, replica_groups=mesh['dp'=2,'seq'=32,'tensor'=2] {'dp'}, use_global_device_ids=true, to_apply=%region_14.15 | all-reduce | flops 2048 | bytes 16384 | tf_op jit(solution)/shard_map/psum | solution.py:103
  177.6 147.5 %psum.31 = f32[2048]{0:T(1024)} all-reduce(f32[2048]{0:T(1024)S(1)} %psum.30), channel_id=1, replica_groups=mesh['dp'=2,'seq'=32,'tensor'=2] {'seq'}, use_global_device_ids=true, to_apply=%region_15.16 | all-reduce | flops 2048 | bytes 16384 | tf_op jit(solution)/shard_map/psum | solution.py:103
  325.1 3.9 multiply_convert_fusion
  329.0 6.7 %fusion.42 = f32[16,512,128]{1,2,0:T(8,128)} fusion(bf16[16,512,128]{1,2,0:T(8,128)(2,1)S(1)} %bitcast.105, bf16[16,512,512]{2,1,0:T(8,128)(2,1)} %copy-done), kind=kOutput, calls=%fused_computation.74 | convolution fusion | flops 1073741824 | bytes 14680064 | tf_op jit(solution)/shard_map/hts,htd->hsd/dot_general | solution.py:119
  335.8 86.6 %while.27 = (s32[]{:T(128)}, f32[16,128,128]{2,1,0:T(8,128)S(1)}, s32[]{:T(128)}, bf16[32,16,128,128]{3,2,1,0:T(8,128)(2,1)}, bf16[32,1]{0,1:T(2,128)(2,1)S(1)},...) while((s32[]{:T(128)}, f32[16,128,128]{2,1,0:T(8,128)S(1)}, s32[]{:T(128)}, ...), condition=%wide.region_12.13_spmd, body=%wide.region_11.12_spmd.sunk | while | flops 786439 | bytes 2621605 | solution.py:31
  424.0 6.2 %add_convert_fusion = bf16[16,512,128]{1,2,0:T(8,128)(2,1)} fusion(f32[16,512,128]{1,2,0:T(8,128)S(1)} %fusion.14, bf16[16,512,128]{1,2,0:T(8,128)(2,1)S(1)} %copy-done.9, bf16[16,512,512]{2,1,0:T(8,128)(2,1)} %copy-done.1), kind=kOutput, calls=%fused_computation.18 | convolution fusion | flops 1075838976 | bytes 16777216 | tf_op jit(solution)/shard_map/hts,hte->hse/dot_general | solution.py:123
  430.3 4.1 copy.98
  434.3 4.2 add_convert_fusion.1
  (118 shorter events, 114.3 us)
Async XLA Ops:
  7.2 106.3 %all-gather.5.cloned.1.call-start = ((), (), s32[]{:S(2)}) async-start(), calls=%async_computation | async-start | bytes 17301504 | tf_op jit(solution)/shard_map/all_gather | solution.py:16
  18.3 4.5 copy-start.2
  19.6 3.9 copy-start.11
  22.8 312.9 %all-gather.7.cloned.1.call-start = ((), (), s32[]{:S(2)}) async-start(), calls=%async_computation.1 | async-start | bytes 17301504 | tf_op jit(solution)/shard_map/all_gather | solution.py:16
  101.3 7.4 %copy-start.3 = (bf16[1,512,2048]{1,2,0:T(8,128)(2,1)S(1)}, bf16[1,512,2048]{1,2,0:T(8,128)(2,1)}, u32[]{:S(2)}) copy-start(bf16[1,512,2048]{1,2,0:T(8,128)(2,1)} %copy-done.2) | copy-start | bytes 6291460
  105.5 3.2 copy-start.1
  123.6 5.4 %copy-start.10 = (f32[2048]{0:T(1024)S(1)}, f32[2048]{0:T(1024)}, u32[]{:S(2)}) copy-start(f32[2048]{0:T(1024)} %param.15) | copy-start | bytes 24580
  142.4 1.4 copy-start.7
  152.7 4.8 %copy-start.5 = (bf16[1,512,2048]{1,2,0:T(8,128)(2,1)S(1)}, bf16[1,512,2048]{1,2,0:T(8,128)(2,1)}, u32[]{:S(2)}) copy-start(bf16[1,512,2048]{1,2,0:T(8,128)(2,1)} %copy.79) | copy-start | bytes 6291460
  157.6 4.8 %copy-start = (bf16[16,512,512]{2,1,0:T(8,128)(2,1)}, bf16[16,512,512]{2,1,0:T(8,128)(2,1)S(1)}, u32[]{:S(2)}) copy-start(bf16[16,512,512]{2,1,0:T(8,128)(2,1)S(1)} %select_convert_fusion) | copy-start | bytes 25165828
  157.6 4.8 %copy-start.8 = (bf16[16,512,128]{1,2,0:T(8,128)(2,1)S(1)}, bf16[16,512,128]{1,2,0:T(8,128)(2,1)}, u32[]{:S(2)}) copy-start(bf16[16,512,128]{1,2,0:T(8,128)(2,1)} %copy-done.7) | copy-start | bytes 6291460
  335.8 86.7 %copy-start.6 = (bf16[1,512,2048]{1,2,0:T(8,128)(2,1)S(1)}, bf16[1,512,2048]{1,2,0:T(8,128)(2,1)}, u32[]{:S(2)}) copy-start(bf16[1,512,2048]{1,2,0:T(8,128)(2,1)} %copy.79) | copy-start | bytes 6291460
  422.5 1.6 copy-start.9
  430.3 4.1 copy-start.4
Sparse Core Ops, SparseCore 0:
  22.9 75.2 all-gather.4
  145.5 151.5 all-gather.6
